TPU v7x, 256 devices: a whole 4x4x8 slice. The times are simulated.
256 devices in a mesh: dom: 8 (over z), feat: 32 (over y, x, core).
Axes of the slice: x: 4, y: 4, z: 8, core: 2. Of those that a mesh axis runs over, the one named last changes fastest.
Arguments:
- features: bfloat16 [32768, 4096], P('dom', 'feat'), may hold values from -6 to 6
- proj_weight: bfloat16 [3, 4096, 256], P(None, 'feat'), may hold values from -0.75 to 0.75
- source_block: int32 [256, 3, 4], P('dom'), may hold values from 0 to 31
- slot_count: int32 [256, 3], P('dom'), may hold values from 1 to 4
- block_pattern: int32 [256, 3, 4, 8, 128], P('dom'), may hold values from 0 to 65535
- node_type: int32 [32768], P(('dom', 'feat')), may hold values from 0 to 2
- type_gain: float32 [3, 256], replicated, may hold values from 0.1 to 1.9
- cotangent: bfloat16 [32768, 256], P(('dom', 'feat')), may hold values from -6 to 6
Outputs:
- activations: bfloat16 [32768, 256], P(('dom', 'feat'))
- weight_grad: float32 [3, 4096, 256], P(None, 'feat')
Inputs may be any that keep to these rules, and one draw needn't show every extreme that they name: `source_block`: a block index within the destination block's own partition. `slot_count`: slots at or past this count are ignored. `block_pattern`: bit j of the word at index w, i marks an edge from source node 16 w + j of the slot's block to node i of the destination block.
All inputs are finite; a program needn't handle non-finite values.
Results may differ from a plain program's by a relative error of at most 0.0055.
Values may be sent and summed in bfloat16 or wider, within the bound.
A program may use at most 128 MiB of HBM per device.

v0:
```python
import jax
import jax.numpy as jnp
from jax import lax
from jax.sharding import PartitionSpec as P

BLK = 128


def unpack_bits(packed):
    shifts = (2 ** jnp.arange(16)).astype(jnp.int32)
    bit_values = packed[..., None] // shifts % 2
    bit_values = jnp.swapaxes(bit_values, -3, -2)
    return bit_values.reshape(packed.shape[:-2] + (packed.shape[-1], packed.shape[-2] * 16))


def silu_grad(pre_act):
    sigmoid_value = jax.nn.sigmoid(pre_act)
    return sigmoid_value * (1.0 + pre_act * (1.0 - sigmoid_value))


def type_rows(node_type, type_gain):
    onehot = (
        node_type[:, None] == jnp.arange(type_gain.shape[0], dtype=jnp.int32)[None, :]
    ).astype(jnp.float32)
    return jnp.sum(onehot[:, :, None] * type_gain[None, :, :], axis=1)


def aggregate(features, source_block, slot_count, block_pattern):
    count_blocks = source_block.shape[0]
    relations = source_block.shape[1]
    slots_each = source_block.shape[2]
    col_width = features.shape[1]
    blocks = features.reshape(count_blocks, BLK, col_width)
    blocks_wide = blocks.astype(jnp.float32)
    live_slots = (
        jnp.arange(slots_each, dtype=jnp.int32)[None, None, :] < slot_count[:, :, None]
    ).astype(jnp.float32)
    mixed_list = []
    for relation in range(relations):
        summed = jnp.zeros((count_blocks, BLK, col_width), jnp.float32)
        degree = jnp.zeros((count_blocks, BLK), jnp.float32)
        for slot_index in range(slots_each):
            adjacency = (
                unpack_bits(block_pattern[:, relation, slot_index]).astype(jnp.float32)
                * live_slots[:, relation, slot_index][:, None, None]
            )
            picked = jnp.take(blocks, source_block[:, relation, slot_index], axis=0)
            summed = summed + jnp.einsum(
                "bij,bjc->bic",
                adjacency.astype(jnp.bfloat16),
                picked,
                preferred_element_type=jnp.float32,
            )
            degree = degree + jnp.sum(adjacency, axis=2)
        mixed_rows = ((blocks_wide + summed) / (1.0 + degree)[:, :, None]).astype(jnp.bfloat16)
        mixed_list.append(mixed_rows.reshape(count_blocks * BLK, col_width))
    return jnp.stack(mixed_list)


def body(
    features, proj_weight, source_block, slot_count, block_pattern, node_type, type_gain, cotangent
):
    mixed_all = aggregate(features, source_block, slot_count, block_pattern)
    rows_now = mixed_all
    pre_act = lax.psum_scatter(
        jnp.einsum("rnc,rch->nh", rows_now, proj_weight, preferred_element_type=jnp.float32),
        "feat",
        scatter_dimension=0,
        tiled=True,
    )
    row_gains = type_rows(node_type, type_gain)
    output = (jax.nn.silu(pre_act) * row_gains).astype(jnp.bfloat16)
    slope_rows = (cotangent.astype(jnp.float32) * row_gains * silu_grad(pre_act)).astype(
        jnp.bfloat16
    )
    rows_now = mixed_all
    local_grad = jnp.einsum(
        "rnc,nh->rch",
        rows_now,
        lax.all_gather(slope_rows, "feat", axis=0, tiled=True),
        preferred_element_type=jnp.float32,
    )
    weight_grad = lax.psum(local_grad, "dom")
    return (output, weight_grad)


def solution(mesh):
    placed = (
        P("dom", "feat"),
        P(None, "feat", None),
        P("dom", None, None),
        P("dom", None),
        P("dom", None, None, None, None),
        P(("dom", "feat")),
        P(),
        P(("dom", "feat"), None),
    )
    return jax.shard_map(
        body,
        mesh=mesh,
        in_specs=placed,
        out_specs=(P(("dom", "feat"), None), P(None, "feat", None)),
        check_vma=False,
    )
```

profile of v0, /device:TPU:1, one launch (start us, length us, event | category | flops | bytes accessed | tf_op | source)
XLA Modules:
  0.0 858.2 jit_solution(449837794035719939)
XLA Ops:
  7.2 2.7 fusion.109
  10.0 1.1 slice_bitcast_fusion.8
  11.2 0.7 compare_and_fusion.8
  11.9 0.7 gather_fusion.2
  12.7 1.7 gather_fusion.1
  14.3 0.7 gather_fusion
  15.1 1.7 gather_fusion.3
  16.8 0.7 pad_clamp_fusion.6
  17.4 1.7 gather_fusion.5
  19.1 1.7 gather_fusion.4
  20.8 0.7 pad_clamp_fusion.4
  21.5 1.7 gather_fusion.6
  23.2 1.6 gather_fusion.7
  24.8 0.6 pad_clamp_fusion.2
  25.5 1.8 gather_fusion.8
  27.2 1.7 gather_fusion.9
  28.9 0.7 pad_clamp_fusion
  29.6 1.7 gather_fusion.10
  31.2 1.6 gather_fusion.11
  32.9 172.3 %fusion.13 = (f32[32,8,128,16]{2,3,1,0:T(8,128)S(1)}, f32[32,8,128,16]{2,3,1,0:T(8,128)S(1)}, f32[32,8,128,16]{2,3,1,0:T(8,128)S(1)}, f32[32,8,128,16]{2,3,1,0:T...) fusion(s32[32,8,128]{2,1,0:T(8,128)} %get-tuple-element.52, ...), kind=kLoop, calls=%fused_computation.78 | loop fusion | flops 79691776 | bytes 18874496 | tf_op jit(solution)/shard_map/convert_element_type | solution.py:44
  205.3 0.4 fusion.38
  205.7 0.4 copy-done.23
  206.5 141.6 %multiply_reduce_fusion.10 = (f32[32,128]{1,0:T(8,128)S(1)}, f32[32,128]{1,0:T(8,128)S(1)}, f32[32,128]{1,0:T(8,128)S(1)}, f32[32,128]{1,0:T(8,128)S(1)}, f32[32,128]{1,0:T(8,128)S(1)}) fusion(f32[32]{0:T(128)S(1)} %get-tuple-element.98, s32[16]{0:T(128)S(1)} %compare_select_fusion.17, s32[32,8,128]{2,1,0:T(8,128)S(1)} %copy-done.31, s32[16]{0:T(128)S(1)} %fusion.117, ...), kind=kLoop, calls=%fused_computation.143 | loop fusion | flops 55029760 | bytes 1393408 | tf_op jit(solution)/shard_map/reduce_sum | solution.py:54
  348.2 84.9 %fusion.21 = (f32[32,8,128,16]{2,3,1,0:T(8,128)S(1)}, f32[32,8,128,16]{2,3,1,0:T(8,128)S(1)}, f32[32,8,128,16]{2,3,1,0:T(8,128)S(1)}, f32[32,8,128,16]{2,3,1,0:T(8,128)S(1)}) fusion(s32[32,8,128]{2,1,0:T(8,128)S(1)} %copy-done.16, s32[32,8,128]{2,1,0:T(8,128)S(1)} %copy-done.11, s32[16]{0:T(128)S(1)} %compare_select_fusion.17, s32[16]{0:T(128)S(1)} %fusion.117, ...), kind=kLoop, calls=%fused_computation.86 | loop fusion | flops 39845888 | bytes 9437312 | tf_op jit(solution)/shard_map/convert_element_type | solution.py:44
  433.1 0.4 fusion.36
  433.5 0.5 copy-done.20
  434.1 43.0 %multiply_reduce_fusion.1 = (f32[32,128]{1,0:T(8,128)S(1)}, f32[32,128]{1,0:T(8,128)S(1)}) fusion(f32[32]{0:T(128)S(1)} %get-tuple-element.90, s32[16]{0:T(128)S(1)} %compare_select_fusion.17, s32[32,8,128]{2,1,0:T(8,128)S(1)} %copy-done.21, s32[16]{0:T(128)S(1)} %fusion.117, s32[32,8,128]{2,1,0:T(8,128)S(1)} %copy-done.20, f32[32]{0:T(128)S(1)} %get-tuple-element.89, ...), kind=kLoop, calls=%fused_computation.134 | loop fusion | flops 22011904 | bytes 557440 | tf_op jit(solution)/shard_map/reduce_sum | solution.py:54
  477.0 0.4 fusion.40
  477.5 0.4 fusion.30
  477.9 0.4 copy-done.10
  478.7 134.1 %multiply_reduce_fusion.11 = (f32[32,128]{1,0:T(8,128)S(1)}, f32[32,128]{1,0:T(8,128)S(1)}, f32[32,128]{1,0:T(8,128)S(1)}, f32[32,128]{1,0:T(8,128)S(1)}, f32[32,128]{1,0:T(8,128)S(1)}) fusion(f32[32]{0:T(128)S(1)} %get-tuple-element.99, s32[16]{0:T(128)S(1)} %compare_select_fusion.17, s32[32,8,128]{2,1,0:T(8,128)S(1)} %copy-done.14, s32[16]{0:T(128)S(1)} %fusion.117, ...), kind=kLoop, calls=%fused_computation.144 | loop fusion | flops 55029760 | bytes 1393408 | tf_op jit(solution)/shard_map/reduce_sum | solution.py:54
  612.8 0.4 fusion.33
  613.2 0.4 fusion.31
  613.6 0.2 copy-done.43
  613.9 0.6 fusion.71
  614.5 0.6 copy-done.3
  615.1 0.6 fusion.73
  615.7 0.6 fusion.75
  616.3 0.6 copy-done.5
  617.0 0.6 fusion.66
  617.5 0.6 copy-done.4
  618.2 0.6 fusion.68
  618.8 0.7 copy-done.6
  619.4 0.6 fusion.64
  620.0 0.7 copy-done.8
  620.6 0.6 fusion.61
  621.2 0.7 copy-done.7
  621.9 0.6 fusion.59
  622.4 0.6 copy-done.9
  623.1 0.6 fusion.57
  623.7 0.6 copy-done.34
  624.3 1.5 fusion.1
  625.9 1.5 fusion.3
  627.5 1.6 fusion.5
  629.1 1.0 copy-done.49
  630.1 3.2 convolution_bitcast_fusion
  633.4 0.6 copy-done.45
  634.0 0.1 multiply_reduce_fusion.12
  634.2 91.4 %reduce-scatter.2.cloned.1.call-done = f32[128,256]{1,0:T(8,128)} async-done(((f32[4096,256]{1,0:T(8,128)}), f32[128,256]{1,0:T(8,128)}) %reduce-scatter.2.cloned.1.call-update) | async-done | bytes 131088 | tf_op jit(solution)/shard_map/reduce_scatter | solution.py:65
  725.5 1.6 multiply_convert_fusion
  727.2 51.6 %all-gather.2.cloned.1.call-done = bf16[4096,256]{1,0:T(8,128)(2,1)} async-done(((bf16[128,256]{1,0:T(8,128)(2,1)}), bf16[4096,256]{1,0:T(8,128)(2,1)}) %all-gather.2.cloned.1.call-update) | async-done | bytes 2097168 | tf_op jit(solution)/shard_map/all_gather | solution.py:80
  778.8 3.7 fusion.42
  782.5 67.2 %all-reduce.2.cloned.1.call-done = f32[3,128,256]{2,1,0:T(8,128)} async-done(((f32[3,128,256]{2,1,0:T(8,128)}), f32[3,128,256]{2,1,0:T(8,128)}) %all-reduce.2.cloned.1.call-update) | async-done | bytes 393232 | tf_op jit(solution)/shard_map/psum | solution.py:83
  849.7 1.8 copy.75
  (101 shorter events, 1.4 us)
Async XLA Ops:
  7.2 622.9 %copy-start = (bf16[3,128,256]{2,1,0:T(8,128)(2,1)S(1)}, bf16[3,128,256]{2,1,0:T(8,128)(2,1)}, u32[]{:S(2)}) copy-start(bf16[3,128,256]{2,1,0:T(8,128)(2,1)} %param.13) | copy-start | bytes 589828
  7.2 2.8 copy-start.2
  7.2 718.3 %reduce-scatter.2.cloned.1.call-start = ((), (), s32[]{:S(2)}) async-start(), calls=%async_computation.1 | async-start | bytes 4325376 | tf_op jit(solution)/shard_map/reduce_scatter | solution.py:65
  10.0 1.2 copy-start.44
  10.0 1.2 copy-start.37
  10.0 1.9 copy-start.1
  205.2 0.9 copy-start.23
  205.2 1.0 copy-start.24
  205.2 1.0 copy-start.25
  205.2 1.1 copy-start.26
  205.2 1.1 copy-start.27
  205.2 1.2 copy-start.28
  205.2 1.2 copy-start.29
  205.2 1.2 copy-start.30
  205.2 1.3 copy-start.31
  205.2 1.3 copy-start.32
  205.3 142.9 %copy-start.11 = (s32[32,8,128]{2,1,0:T(8,128)S(1)}, s32[32,8,128]{2,1,0:T(8,128)}, u32[]{:S(2)}) copy-start(s32[32,8,128]{2,1,0:T(8,128)} %get-tuple-element.43) | copy-start | bytes 393220
  205.3 142.9 %copy-start.16 = (s32[32,8,128]{2,1,0:T(8,128)S(1)}, s32[32,8,128]{2,1,0:T(8,128)}, u32[]{:S(2)}) copy-start(s32[32,8,128]{2,1,0:T(8,128)} %get-tuple-element.59) | copy-start | bytes 393220
  205.3 142.9 %copy-start.19 = (s32[32,8,128]{2,1,0:T(8,128)S(1)}, s32[32,8,128]{2,1,0:T(8,128)}, u32[]{:S(2)}) copy-start(s32[32,8,128]{2,1,0:T(8,128)} %get-tuple-element.50) | copy-start | bytes 393220
  205.3 142.9 %copy-start.22 = (s32[32,8,128]{2,1,0:T(8,128)S(1)}, s32[32,8,128]{2,1,0:T(8,128)}, u32[]{:S(2)}) copy-start(s32[32,8,128]{2,1,0:T(8,128)} %get-tuple-element.63) | copy-start | bytes 393220
  433.1 0.9 copy-start.20
  433.1 1.0 copy-start.21
  477.4 0.9 copy-start.10
  477.4 1.0 copy-start.12
  477.5 1.0 copy-start.13
  477.5 1.1 copy-start.14
  477.5 1.1 copy-start.15
  477.5 1.2 copy-start.17
  477.5 1.2 copy-start.18
  613.2 0.7 copy-start.43
  613.9 1.2 copy-start.3
  613.9 1.2 copy-start.42
  615.1 0.6 copy-start.41
  615.7 1.2 copy-start.5
  615.7 1.2 copy-start.40
  617.0 1.2 copy-start.4
  617.0 1.2 copy-start.39
  618.2 1.2 copy-start.6
  619.4 1.2 copy-start.8
  620.6 1.2 copy-start.7
  621.9 1.2 copy-start.9
  623.1 1.2 copy-start.34
  623.1 1.2 copy-start.48
  624.3 1.6 copy-start.33
  624.3 1.6 copy-start.47
  625.9 1.6 copy-start.35
  625.9 1.6 copy-start.46
  629.1 1.0 copy-start.49
  633.3 0.7 copy-start.45
  633.3 0.7 copy-start.38
  633.3 92.2 %copy-start.36 = (bf16[128,256]{1,0:T(8,128)(2,1)S(1)}, bf16[128,256]{1,0:T(8,128)(2,1)}, u32[]{:S(2)}) copy-start(bf16[128,256]{1,0:T(8,128)(2,1)} %param.19) | copy-start | bytes 196612
  633.4 145.4 %all-gather.2.cloned.1.call-start = ((), (), s32[]{:S(2)}) async-start(), calls=%async_computation.2 | async-start | bytes 2162688 | tf_op jit(solution)/shard_map/all_gather | solution.py:80
  727.2 122.6 %all-reduce.2.cloned.1.call-start = ((), (), s32[]{:S(2)}) async-start(), calls=%async_computation.3 | async-start | bytes 786432 | tf_op jit(solution)/shard_map/psum | solution.py:83
Sparse Core Ops, SparseCore 0:
  633.5 91.9 reduce-scatter.1
  728.7 50.0 all-gather.1
  782.6 67.0 all-reduce.1
where the time goes:
time: 866 us; the launch traced here: 858 us
  other arithmetic  586 us (68%)
  waiting for transfers between devices  210 us (24%)
  local copies, waits for them, and re-layouts  30.5 us (4%)
  matrix products  16.7 us (2%)
  between operations  14.6 us (2%)
    reduce_sum x3, other arithmetic, aggregate(): degree = degree + jnp.sum(adjacency, axis=2)  319 us
    convert_element_type x2, other arithmetic, aggregate(): unpack_bits(block_pattern[:, relation, slot_index]).astype(jnp.float32)  257 us
    reduce_scatter x1, waiting for transfers between devices, body(): lax.psum_scatter(jnp.einsum('rnc,rch->nh', rows_now, proj_weight, preferr...  91.4 us
    psum x1, waiting for transfers between devices, body(): weight_grad = lax.psum(local_grad, 'dom')  67.2 us
    all_gather x1, waiting for transfers between devices, body(): lax.all_gather(slope_rows, 'feat', axis=0, tiled=True)  51.6 us
    gather x12, local copies, waits for them, and re-layouts, aggregate(): picked = jnp.take(blocks, source_block[:, relation, slot_index], axis=0)  18.3 us
  transfers between devices with their start and end apart: 3, of which 3 were waited for; matrix products, arithmetic and copies ran while one was open for 0% of the time, Pallas kernels for 0%

commit v1 on v0

v1 whole, which is shorter than its diff:
```python
import functools

import jax
import jax.numpy as jnp
from jax import lax
from jax.experimental import pallas as pl
from jax.experimental.pallas import tpu as pltpu
from jax.sharding import PartitionSpec as P

MESH = pl.DeviceIdType.MESH
F32 = jnp.float32
BF16 = jnp.bfloat16
BLK = 128
REL = 3
SLOTS = 4
PB = 32
HID = 256
NZ = 8
PART = REL * BLK // NZ


def kernel(
    feat_ref,
    weight_ref,
    source_ref,
    count_ref,
    pattern_ref,
    type_ref,
    gain_ref,
    cot_ref,
    act_ref,
    grad_ref,
    self_t,
    perm_t,
    weight_t,
    mixed_t,
    own_part,
    pair_out,
    pair_in,
    rs_out,
    rs_in,
    slope_all,
    grad_acc,
    wg_out,
    wg_in,
    wg_all,
    pair_send,
    pair_recv,
    rs_send,
    rs_recv,
    agx_send,
    agx_recv,
    agy_send,
    agy_recv,
    core_send,
    core_recv,
    zs_send,
    zs_recv,
    zb_send,
    zb_recv,
):
    dom = lax.axis_index("dom")
    me = lax.axis_index("feat")
    core = me % 2
    chip = me // 2
    x = chip % 4
    y = chip // 4
    partner = me + 1 - 2 * core

    def at_feat(dest):
        return (dom, dest)

    def device_at(dy, dx):
        return (((y + dy) % 4) * 4 + (x + dx) % 4) * 2 + core

    barrier = pltpu.get_barrier_semaphore()

    def greet(dest):
        pl.semaphore_signal(barrier, inc=1, device_id=dest, device_id_type=MESH)

    greet(at_feat(partner))
    for off in range(1, 16):
        greet(at_feat(device_at(off // 4, off % 4)))
    for dz in range(1, NZ):
        greet(((dom + dz) % NZ, me))

    row = lax.broadcasted_iota(jnp.int32, (BLK, BLK), 0)
    col = lax.broadcasted_iota(jnp.int32, (BLK, BLK), 1)
    scale = 1.0 / (jnp.int32(1) << (col // 8)).astype(F32)
    perm = jnp.where(row == (col % 8) * 16 + col // 8, scale, 0.0).astype(BF16)
    eye = jnp.where(row == col, 1.0, 0.0).astype(BF16)

    for r in range(REL):
        for half in range(2):
            piece = weight_ref[r, :, half * BLK:(half + 1) * BLK]
            weight_t[half * BLK:(half + 1) * BLK, r * BLK:(r + 1) * BLK] = (
                piece.astype(F32).T.astype(BF16)
            )

    def prepare(i, carry):
        for k in range(4):
            b = i * 4 + k
            rows = feat_ref[pl.ds(pl.multiple_of(b * BLK, BLK), BLK), :]
            flipped = lax.dot_general(
                eye, rows, (((1,), (1,)), ((), ())), preferred_element_type=F32
            ).astype(BF16)
            self_t[b] = flipped
            perm_t[b] = jnp.dot(flipped, perm, preferred_element_type=F32).astype(BF16)
        return carry

    lax.fori_loop(0, PB // 4, prepare, 0)

    def mix(b):
        own_rows = self_t[b].astype(F32)
        for r in range(REL):
            count = count_ref[b, r]
            tiles = []
            gathered = []
            degree = None
            for s in range(SLOTS):
                words = pattern_ref[b, r, s]
                if s > 0:
                    words = words & jnp.where(s < count, jnp.int32(65535), jnp.int32(0))
                bits = lax.population_count(words)
                degree = bits if degree is None else degree + bits
                for j in range(16):
                    tiles.append((words & (1 << j)).astype(F32))
                gathered.append(perm_t[source_ref[b, r, s]])
            adj = jnp.concatenate(tiles, axis=0).astype(BF16)
            sources = jnp.concatenate(gathered, axis=1)
            summed = jnp.dot(sources, adj, preferred_element_type=F32)
            total = 1.0 + jnp.sum(degree.astype(F32), axis=0, keepdims=True)
            mixed_t[b, r * BLK:(r + 1) * BLK, :] = ((own_rows + summed) * (1.0 / total)).astype(BF16)

    def pair_copy(step):
        return pltpu.make_async_remote_copy(
            src_ref=pair_out.at[step],
            dst_ref=pair_in.at[step],
            send_sem=pair_send.at[step],
            recv_sem=pair_recv.at[step],
            device_id=at_feat(partner),
            device_id_type=MESH,
        )

    def rs_copy(step):
        off = 15 - step
        return pltpu.make_async_remote_copy(
            src_ref=rs_out.at[step],
            dst_ref=rs_in.at[step],
            send_sem=rs_send.at[step],
            recv_sem=rs_recv.at[step],
            device_id=at_feat(device_at(off // 4, off % 4)),
            device_id_type=MESH,
        )

    def project(step):
        off = 15 - step
        mine = device_at(off // 4, off % 4)
        other = mine + 1 - 2 * core
        mix(mine)
        mix(other)
        both = jnp.concatenate([mixed_t[mine], mixed_t[other]], axis=1)
        part = jnp.dot(weight_t[...], both, preferred_element_type=F32)
        own_part[step % 2] = part[:, :BLK]
        pair_out[step] = part[:, BLK:].astype(BF16)

    def pair_sum(step):
        pair_copy(step).wait_recv()
        return own_part[step % 2] + pair_in[step].astype(F32)

    project(0)
    pl.semaphore_wait(barrier, 1 + 15 + NZ - 1)
    pair_copy(0).start()

    def stage(step, carry):
        project(step)
        pair_copy(step).start()
        rs_out[step - 1] = pair_sum(step - 1).astype(BF16)
        rs_copy(step - 1).start()
        return carry

    lax.fori_loop(1, 16, stage, 0)
    total = pair_sum(15)
    for step in range(15):
        rs_copy(step).wait_recv()
        total = total + rs_in[step].astype(F32)

    types = jnp.broadcast_to(type_ref[...].astype(F32), (BLK, BLK)).T
    for half in range(2):
        cols = slice(half * BLK, (half + 1) * BLK)
        pre = total[cols].T
        gains = gain_ref[:, cols]
        gain = jnp.where(types == 0.0, gains[0:1], jnp.where(types == 1.0, gains[1:2], gains[2:3]))
        sig = jax.nn.sigmoid(pre)
        act_ref[:, cols] = (pre * sig * gain).astype(BF16)
        slope = cot_ref[:, cols].astype(F32) * gain * (sig * (1.0 + pre * (1.0 - sig)))
        slope_all[me, :, cols] = slope.astype(BF16)

    def to_core(block, slot):
        return pltpu.make_async_remote_copy(
            src_ref=slope_all.at[block],
            dst_ref=slope_all.at[block],
            send_sem=core_send.at[slot],
            recv_sem=core_recv.at[slot],
            device_id=at_feat(partner),
            device_id_type=MESH,
        )

    def over_x(block, line, dx):
        return pltpu.make_async_remote_copy(
            src_ref=slope_all.at[block, pl.ds(64 if line[1] else 0, 64)],
            dst_ref=slope_all.at[block, pl.ds(64 if line[1] else 0, 64)],
            send_sem=agx_send.at[line[0] + 4 * line[1], dx],
            recv_sem=agx_recv.at[line[0] + 4 * line[1], dx],
            device_id=at_feat(device_at(0, dx)),
            device_id_type=MESH,
        )

    def over_y(block, line, dy):
        return pltpu.make_async_remote_copy(
            src_ref=slope_all.at[block, pl.ds(0 if line[1] else 64, 64)],
            dst_ref=slope_all.at[block, pl.ds(0 if line[1] else 64, 64)],
            send_sem=agy_send.at[line[0] + 4 * line[1], dy],
            recv_sem=agy_recv.at[line[0] + 4 * line[1], dy],
            device_id=at_feat(device_at(dy, 0)),
            device_id_type=MESH,
        )

    hops = (1, 3, 2)
    for d in hops:
        over_x(me, (0, 0), d).start()
        over_y(me, (0, 0), d).start()
    for d in hops:
        over_x(me, (0, 1), d).start()
        over_y(me, (0, 1), d).start()
    to_core(me, 0).start()
    for d in hops:
        across = device_at(0, 4 - d)
        over_x(across, (0, 0), d).wait_recv()
        for e in hops:
            over_y(across, (d, 1), e).start()
        down = device_at(4 - d, 0)
        over_y(down, (0, 0), d).wait_recv()
        for e in hops:
            over_x(down, (d, 1), e).start()

    def arrived(dy, dx):
        block = device_at(4 - dy, 4 - dx)
        if dy == 0:
            over_x(block, (0, 1), dx).wait_recv()
        elif dx == 0:
            over_y(block, (0, 1), dy).wait_recv()
        else:
            over_y(block, (dx, 1), dy).wait_recv()
            over_x(block, (dy, 1), dx).wait_recv()
        return block

    def add_grad(block, slot):
        twin = block + 1 - 2 * core
        to_core(twin, slot).wait_recv()
        lhs = jnp.concatenate([mixed_t[block], mixed_t[twin]], axis=1)
        rhs = jnp.concatenate([slope_all[block], slope_all[twin]], axis=0)
        return jnp.dot(lhs, rhs, preferred_element_type=F32)

    order = [(0, 1), (0, 3), (1, 0), (3, 0), (0, 2), (2, 0), (1, 1), (1, 3), (3, 1), (3, 3),
             (1, 2), (2, 1), (3, 2), (2, 3), (2, 2)]
    before = (me, 0)
    for n, (dy, dx) in enumerate(order):
        block = arrived(dy, dx)
        to_core(block, dy * 4 + dx).start()
        if n == 0:
            grad_acc[...] = add_grad(*before)
        else:
            grad_acc[...] += add_grad(*before)
        before = (block, dy * 4 + dx)
    grad_acc[...] += add_grad(*before)

    def scatter(dz):
        return pltpu.make_async_remote_copy(
            src_ref=wg_out.at[(dom + dz) % NZ],
            dst_ref=wg_in.at[dz],
            send_sem=zs_send.at[dz],
            recv_sem=zs_recv.at[dz],
            device_id=((dom + dz) % NZ, me),
            device_id_type=MESH,
        )

    def spread(dz, part):
        return pltpu.make_async_remote_copy(
            src_ref=wg_all.at[part],
            dst_ref=wg_all.at[part],
            send_sem=zb_send.at[dz],
            recv_sem=zb_recv.at[dz],
            device_id=((dom + dz) % NZ, me),
            device_id_type=MESH,
        )

    for p in range(NZ):
        wg_out[p] = grad_acc[p * PART:(p + 1) * PART, :].astype(BF16)
    zorder = (4, 3, 5, 2, 6, 1, 7)
    for dz in zorder:
        scatter(dz).start()
    own = grad_acc[pl.ds(pl.multiple_of(dom * PART, 8), PART), :]
    for dz in reversed(zorder):
        scatter(dz).wait_recv()
        own = own + wg_in[dz].astype(F32)
    wg_all[dom] = own.astype(BF16)
    for dz in zorder:
        spread(dz, dom).start()
    grad_ref[pl.ds(pl.multiple_of(dom * PART, 8), PART), :] = own.astype(BF16).astype(F32)
    for dz in reversed(zorder):
        part = (dom + NZ - dz) % NZ
        spread(dz, part).wait_recv()
        grad_ref[pl.ds(pl.multiple_of(part * PART, 8), PART), :] = wg_all[part].astype(F32)

    def drain(step, carry):
        pair_copy(step).wait_send()
        return carry

    lax.fori_loop(0, 16, drain, 0)

    def drain_rs(step, carry):
        rs_copy(step).wait_send()
        return carry

    lax.fori_loop(0, 15, drain_rs, 0)
    for d in hops:
        over_x(me, (0, 0), d).wait_send()
        over_y(me, (0, 0), d).wait_send()
        for k in range(4):
            over_x(me, (k, 1), d).wait_send()
            over_y(me, (k, 1), d).wait_send()
    for slot in range(16):
        to_core(me, slot).wait_send()
    for dz in range(1, NZ):
        scatter(dz).wait_send()
        spread(dz, dom).wait_send()


def body(
    features, proj_weight, source_block, slot_count, block_pattern, node_type, type_gain, cotangent
):
    vmem = pl.BlockSpec(memory_space=pltpu.VMEM)
    smem = pl.BlockSpec(memory_space=pltpu.SMEM)
    activations, grad = pl.pallas_call(
        kernel,
        out_shape=(
            jax.ShapeDtypeStruct((BLK, HID), BF16),
            jax.ShapeDtypeStruct((REL * BLK, HID), F32),
        ),
        in_specs=[vmem, vmem, smem, smem, vmem, vmem, vmem, vmem],
        out_specs=(vmem, vmem),
        scratch_shapes=[
            pltpu.VMEM((PB, BLK, BLK), BF16),
            pltpu.VMEM((PB, BLK, BLK), BF16),
            pltpu.VMEM((HID, REL * BLK), BF16),
            pltpu.VMEM((PB, REL * BLK, BLK), BF16),
            pltpu.VMEM((2, HID, BLK), F32),
            pltpu.VMEM((16, HID, BLK), BF16),
            pltpu.VMEM((16, HID, BLK), BF16),
            pltpu.VMEM((16, HID, BLK), BF16),
            pltpu.VMEM((16, HID, BLK), BF16),
            pltpu.VMEM((PB, BLK, HID), BF16),
            pltpu.VMEM((REL * BLK, HID), F32),
            pltpu.VMEM((NZ, PART, HID), BF16),
            pltpu.VMEM((NZ, PART, HID), BF16),
            pltpu.VMEM((NZ, PART, HID), BF16),
            pltpu.SemaphoreType.DMA((16,)),
            pltpu.SemaphoreType.DMA((16,)),
            pltpu.SemaphoreType.DMA((16,)),
            pltpu.SemaphoreType.DMA((16,)),
            pltpu.SemaphoreType.DMA((8, 4)),
            pltpu.SemaphoreType.DMA((8, 4)),
            pltpu.SemaphoreType.DMA((8, 4)),
            pltpu.SemaphoreType.DMA((8, 4)),
            pltpu.SemaphoreType.DMA((16,)),
            pltpu.SemaphoreType.DMA((16,)),
            pltpu.SemaphoreType.DMA((NZ,)),
            pltpu.SemaphoreType.DMA((NZ,)),
            pltpu.SemaphoreType.DMA((NZ,)),
            pltpu.SemaphoreType.DMA((NZ,)),
        ],
        compiler_params=pltpu.CompilerParams(
            collective_id=0, has_side_effects=True, vmem_limit_bytes=60 * 1024 * 1024
        ),
        name="graph_conv",
    )(
        features,
        proj_weight,
        source_block,
        slot_count,
        block_pattern,
        node_type.reshape(1, BLK),
        type_gain,
        cotangent,
    )
    return activations, grad.reshape(REL, BLK, HID)


def solution(mesh):
    placed = (
        P("dom", "feat"),
        P(None, "feat", None),
        P("dom", None, None),
        P("dom", None),
        P("dom", None, None, None, None),
        P(("dom", "feat")),
        P(),
        P(("dom", "feat"), None),
    )
    return jax.shard_map(
        body,
        mesh=mesh,
        in_specs=placed,
        out_specs=(P(("dom", "feat"), None), P(None, "feat", None)),
        check_vma=False,
    )
```

time: 866 us -> 70.7 us (0.08)
  the two profiles are of different devices: /device:TPU:1 before, /device:TPU:8 now
where the time goes in v1:
time: 70.7 us; the launch traced here: 70.5 us
  Pallas kernels  63.8 us (90%)
  local copies, waits for them, and re-layouts  6.03 us (9%)
    pallas_call x1, Pallas kernels, body(): pl.pallas_call(kernel, out_shape=(jax.ShapeDtypeStruct((BLK, HID), BF16),...  63.8 us
    unnamed x4, local copies, waits for them, and re-layouts  6.03 us

profile of v1, /device:TPU:8, one launch (start us, length us, event | category | flops | bytes accessed | tf_op | source)
XLA Modules:
  0.0 70.5 jit_solution(11521609470161333010)
XLA Ops:
  0.6 1.4 %copy.11.count_ref = s32[32,3]{1,0:T(8,128)} copy(s32[32,3]{0,1:T(4,128)} %param.11) | data formatting | bytes 768 | tf_op args[3]
  2.0 1.4 %copy.10.source_ref = s32[32,3,4]{2,1,0:T(4,128)} copy(s32[32,3,4]{0,2,1:T(4,128)} %param.10) | data formatting | bytes 3072 | tf_op args[2]
  3.4 63.8 %graph_conv.1 = (bf16[128,256]{1,0:T(8,128)(2,1)}, f32[384,256]{1,0:T(8,128)}) custom-call(bf16[4096,128]{1,0:T(8,128)(2,1)} %feat_ref.1, bf16[3,128,256]{2,1,0:T(8,128)(2,1)} %weight_ref.1, s32[32,3,4]{2,1,0:T(4,128)} %copy.10.source_ref, s32[32,3]{1,0:T(8,128)} %copy.11.count_ref, s32[32,3,4,8,128]{4,3,2,1,0:T(8,128)} %pattern_ref.1, s32[1,128]{1,0:T(1,128)} %bitcast.3, ...), custom_call_target="tpu_custom_call" | custom-call | tf_op jit(solution)/shard_map/graph_conv/pallas_call | solution.py:345
  67.2 1.5 %copy.14 = bf16[128,256]{1,0:T(8,128)(2,1)} copy(bf16[128,256]{1,0:T(8,128)(2,1)} %get-tuple-element.8) | data formatting | bytes 131072
  68.7 1.8 %copy.15 = f32[3,128,256]{2,1,0:T(8,128)} copy(f32[3,128,256]{2,1,0:T(8,128)} %bitcast.2) | data formatting | bytes 786432

commit v2 on v1

v2 whole, which is shorter than its diff:
```python
import functools

import jax
import jax.numpy as jnp
from jax import lax
from jax.experimental import pallas as pl
from jax.experimental.pallas import tpu as pltpu
from jax.sharding import PartitionSpec as P

MESH = pl.DeviceIdType.MESH
F32 = jnp.float32
BF16 = jnp.bfloat16
BLK = 128
REL = 3
NTYPES = 3
SLOTS = 4
PB = 32
HID = 256
NZ = 8
DXS = (2, 3, 1, 0)
PART = REL * BLK // NZ


def kernel(
    feat_hbm,
    weight_hbm,
    source_hbm,
    count_hbm,
    pattern_hbm,
    type_hbm,
    gain_hbm,
    cot_hbm,
    act_ref,
    wg_all,
    feat_ref,
    weight_ref,
    source_ref,
    count_ref,
    pattern_ref,
    type_ref,
    gain_ref,
    cot_ref,
    load_sem,
    self_t,
    perm_t,
    weight_t,
    mixed_t,
    own_part,
    keep_top,
    pair_out,
    pair_in,
    x_out,
    x_in,
    y_out,
    y_in,
    turn_out,
    turn_in,
    slope_all,
    grad_acc,
    wg_out,
    wg_in,
    pair_send,
    pair_recv,
    x_send,
    x_recv,
    y_send,
    y_recv,
    turn_send,
    turn_recv,
    agx_send,
    agx_recv,
    agy_send,
    agy_recv,
    core_send,
    core_recv,
    zs_send,
    zs_recv,
    zb_send,
    zb_recv,
):
    dom = lax.axis_index("dom")
    me = lax.axis_index("feat")
    core = me % 2
    chip = me // 2
    x = chip % 4
    y = chip // 4
    partner = me + 1 - 2 * core

    def at_feat(dest):
        return (dom, dest)

    def device_at(dy, dx):
        return (((y + dy) % 4) * 4 + (x + dx) % 4) * 2 + core

    loads = [
        pltpu.make_async_copy(src, dst, load_sem.at[n])
        for n, (src, dst) in enumerate((
            (feat_hbm, feat_ref),
            (weight_hbm, weight_ref),
            (source_hbm, source_ref),
            (count_hbm, count_ref),
            (pattern_hbm, pattern_ref),
            (type_hbm, type_ref),
            (gain_hbm, gain_ref),
            (cot_hbm, cot_ref),
        ))
    ]
    for load in loads:
        load.start()

    barrier = pltpu.get_barrier_semaphore()

    def greet(dest):
        pl.semaphore_signal(barrier, inc=1, device_id=dest, device_id_type=MESH)

    greet(at_feat(partner))
    for off in range(1, 16):
        greet(at_feat(device_at(off // 4, off % 4)))
    for dz in range(1, NZ):
        greet(((dom + dz) % NZ, me))

    row = lax.broadcasted_iota(jnp.int32, (BLK, BLK), 0)
    col = lax.broadcasted_iota(jnp.int32, (BLK, BLK), 1)
    scale = 1.0 / (jnp.int32(1) << (col // 8)).astype(F32)
    perm = jnp.where(row == (col % 8) * 16 + col // 8, scale, 0.0).astype(BF16)
    eye = jnp.where(row == col, 1.0, 0.0).astype(BF16)

    loads[0].wait()
    loads[1].wait()
    for r in range(REL):
        for half in range(2):
            piece = weight_ref[r, :, half * BLK:(half + 1) * BLK]
            weight_t[half * BLK:(half + 1) * BLK, r * BLK:(r + 1) * BLK] = (
                piece.astype(F32).T.astype(BF16)
            )

    def prepare(i, carry):
        for k in range(4):
            b = i * 4 + k
            rows = feat_ref[pl.ds(pl.multiple_of(b * BLK, BLK), BLK), :]
            flipped = lax.dot_general(
                eye, rows, (((1,), (1,)), ((), ())), preferred_element_type=F32
            ).astype(BF16)
            self_t[b] = flipped
            perm_t[b] = jnp.dot(flipped, perm, preferred_element_type=F32).astype(BF16)
        return carry

    lax.fori_loop(0, PB // 4, prepare, 0)
    for load in loads[2:]:
        load.wait()

    def mix(b):
        own_rows = self_t[b].astype(F32)
        for r in range(REL):
            count = count_ref[r, b]
            tiles = []
            gathered = []
            degree = None
            for s in range(SLOTS):
                words = pattern_ref[b, r, s]
                if s > 0:
                    words = words & jnp.where(s < count, jnp.int32(65535), jnp.int32(0))
                bits = lax.population_count(words)
                degree = bits if degree is None else degree + bits
                for j in range(16):
                    tiles.append((words & (1 << j)).astype(F32))
                gathered.append(perm_t[source_ref[r, s, b]])
            adj = jnp.concatenate(tiles, axis=0).astype(BF16)
            sources = jnp.concatenate(gathered, axis=1)
            summed = jnp.dot(sources, adj, preferred_element_type=F32)
            total = 1.0 + jnp.sum(degree.astype(F32), axis=0, keepdims=True)
            mixed_t[b, r * BLK:(r + 1) * BLK, :] = ((own_rows + summed) * (1.0 / total)).astype(BF16)

    def pair_copy(step):
        return pltpu.make_async_remote_copy(
            src_ref=pair_out.at[step],
            dst_ref=pair_in.at[step],
            send_sem=pair_send.at[step],
            recv_sem=pair_recv.at[step],
            device_id=at_feat(partner),
            device_id_type=MESH,
        )

    def shift(n):
        return 2 + n - 3 * (n // 2) - 2 * (n // 3)

    def offset(step):
        group, k = step // 4, step % 4
        return shift(group), shift(k)

    def target(step):
        dy, dx = offset(step)
        return device_at(dy, dx)

    def x_copy(step, dx):
        return pltpu.make_async_remote_copy(
            src_ref=x_out.at[step],
            dst_ref=x_in.at[step],
            send_sem=x_send.at[step],
            recv_sem=x_recv.at[step],
            device_id=at_feat(device_at(0, dx)),
            device_id_type=MESH,
        )

    def y_copy(step, dy):
        return pltpu.make_async_remote_copy(
            src_ref=y_out.at[step],
            dst_ref=y_in.at[step],
            send_sem=y_send.at[step],
            recv_sem=y_recv.at[step],
            device_id=at_feat(device_at(dy, 0)),
            device_id_type=MESH,
        )

    def turn_copy(kind, slot, d):
        return pltpu.make_async_remote_copy(
            src_ref=turn_out.at[kind, slot],
            dst_ref=turn_in.at[kind, slot],
            send_sem=turn_send.at[kind, slot],
            recv_sem=turn_recv.at[kind, slot],
            device_id=at_feat(device_at(d, 0) if kind == 0 else device_at(0, d)),
            device_id_type=MESH,
        )

    def project(step):
        mine = target(step)
        other = mine + 1 - 2 * core
        mix(mine)
        mix(other)
        both = jnp.concatenate([mixed_t[mine], mixed_t[other]], axis=1)
        part = jnp.dot(weight_t[...], both, preferred_element_type=F32)
        own_part[step] = part[:, :BLK]
        pair_out[step] = part[:, BLK:].astype(BF16)
        pair_copy(step).start()

    def top_sum(step):
        return own_part[step, :BLK] + pair_in[step, :BLK].astype(F32)

    def low_sum(step):
        return own_part[step, BLK:] + pair_in[step, BLK:].astype(F32)

    def send_top(step, k):
        x_out[step] = top_sum(step).astype(BF16)
        x_copy(step, DXS[k]).start()

    def send_low(step, dy):
        y_out[step] = low_sum(step).astype(BF16)
        y_copy(step, dy).start()

    def row_sum(group, mine):
        for k in range(3):
            x_copy(4 * group + k, DXS[k]).wait_recv()
            mine = mine + x_in[4 * group + k].astype(F32)
        return mine

    def send_row(group, dy):
        turn_out[0, group] = row_sum(group, keep_top[group]).astype(BF16)
        turn_copy(0, group, dy).start()

    def column_sum(k, mine):
        for group in range(3):
            y_copy(4 * group + k, 1).wait_recv()
            mine = mine + y_in[4 * group + k].astype(F32)
        return mine

    pl.semaphore_wait(barrier, 1 + 15 + NZ - 1)
    project(0)
    project(1)

    def four(group, carry):
        dy = shift(group)
        for k in range(4):
            step = 4 * group + k
            project(step + 2)
            pair_copy(step).wait_recv()
            if k < 3:
                send_top(step, k)
            else:
                keep_top[group] = top_sum(step)
            send_low(step, dy)
            if k == 2:
                @pl.when(group > 0)
                def _():
                    send_row(group - 1, shift(group - 1))
        return carry

    lax.fori_loop(0, 3, four, 0)
    for k in range(4):
        step = 12 + k
        if k < 2:
            project(step + 2)
        pair_copy(step).wait_recv()
        if k < 3:
            send_top(step, k)
            turn_out[1, k] = column_sum(k, low_sum(step)).astype(BF16)
            turn_copy(1, k, DXS[k]).start()
        if k == 2:
            send_row(2, 1)
    top = row_sum(3, top_sum(15))
    low = column_sum(3, low_sum(15))
    for slot in range(3):
        turn_copy(0, slot, 1).wait_recv()
        top = top + turn_in[0, slot].astype(F32)
        turn_copy(1, slot, 1).wait_recv()
        low = low + turn_in[1, slot].astype(F32)

    types = jnp.broadcast_to(type_ref[...].astype(F32), (BLK, BLK)).T
    for half in range(2):
        cols = slice(half * BLK, (half + 1) * BLK)
        pre = (top, low)[half].T
        gains = gain_ref[:, cols]
        gain = jnp.where(types == 0.0, gains[0:1], jnp.where(types == 1.0, gains[1:2], gains[2:3]))
        sig = jax.nn.sigmoid(pre)
        act_ref[:, cols] = (pre * sig * gain).astype(BF16)
        slope = cot_ref[:, cols].astype(F32) * gain * (sig * (1.0 + pre * (1.0 - sig)))
        slope_all[half, me] = slope.astype(BF16)

    def to_core(half, block, slot):
        return pltpu.make_async_remote_copy(
            src_ref=slope_all.at[half, block],
            dst_ref=slope_all.at[half, block],
            send_sem=core_send.at[half, slot],
            recv_sem=core_recv.at[half, slot],
            device_id=at_feat(partner),
            device_id_type=MESH,
        )

    def over_x(half, block, line, dx):
        rows = pl.ds(64 if line > 0 else 0, 64)
        return pltpu.make_async_remote_copy(
            src_ref=slope_all.at[half, block, rows],
            dst_ref=slope_all.at[half, block, rows],
            send_sem=agx_send.at[half, line, dx],
            recv_sem=agx_recv.at[half, line, dx],
            device_id=at_feat(device_at(0, dx)),
            device_id_type=MESH,
        )

    def over_y(half, block, line, dy):
        rows = pl.ds(0 if line > 0 else 64, 64)
        return pltpu.make_async_remote_copy(
            src_ref=slope_all.at[half, block, rows],
            dst_ref=slope_all.at[half, block, rows],
            send_sem=agy_send.at[half, line, dy],
            recv_sem=agy_recv.at[half, line, dy],
            device_id=at_feat(device_at(dy, 0)),
            device_id_type=MESH,
        )

    for half in range(2):
        for line in range(2):
            for d in DXS[:3]:
                over_x(half, me, line, d).start()
                over_y(half, me, line, d).start()
        to_core(half, me, 0).start()

    def forward(half):
        for d in (1, 3, 2):
            across = device_at(0, 4 - d)
            over_x(half, across, 0, d).wait_recv()
            for e in DXS[:3]:
                over_y(half, across, 1 + d, e).start()
            down = device_at(4 - d, 0)
            over_y(half, down, 0, d).wait_recv()
            for e in DXS[:3]:
                over_x(half, down, 1 + d, e).start()

    def arrived(half, dy, dx):
        block = device_at(4 - dy, 4 - dx)
        if dx > 0:
            over_x(half, block, 1 + dy, dx).wait_recv()
        if dy > 0:
            over_y(half, block, 1 + dx, dy).wait_recv()
        return block

    def add_grad(half, block, slot):
        twin = block + 1 - 2 * core
        to_core(half, twin, slot).wait_recv()
        lhs = jnp.concatenate([mixed_t[block], mixed_t[twin]], axis=1)
        rhs = jnp.concatenate([slope_all[half, block], slope_all[half, twin]], axis=0)
        return jnp.dot(lhs, rhs, preferred_element_type=F32)

    order = [(0, 1), (0, 3), (1, 0), (3, 0), (0, 2), (2, 0), (1, 1), (1, 3), (3, 1), (3, 3),
             (1, 2), (2, 1), (3, 2), (2, 3), (2, 2)]

    def relay(half):
        for dy, dx in order:
            block = arrived(half, dy, dx)
            to_core(half, block, dy * 4 + dx).start()

    def gradient(half):
        grad_acc[...] = add_grad(half, me, 0)
        for dy, dx in order:
            grad_acc[...] += add_grad(half, device_at(4 - dy, 4 - dx), dy * 4 + dx)

    def scatter(half, dz):
        return pltpu.make_async_remote_copy(
            src_ref=wg_out.at[half, (dom + dz) % NZ],
            dst_ref=wg_in.at[half, dz],
            send_sem=zs_send.at[half, dz],
            recv_sem=zs_recv.at[half, dz],
            device_id=((dom + dz) % NZ, me),
            device_id_type=MESH,
        )

    def spread(half, dz, part):
        return pltpu.make_async_remote_copy(
            src_ref=wg_all.at[half, part],
            dst_ref=wg_all.at[half, part],
            send_sem=zb_send.at[half, dz],
            recv_sem=zb_recv.at[half, dz],
            device_id=((dom + dz) % NZ, me),
            device_id_type=MESH,
        )

    zorder = (4, 3, 5, 2, 6, 1, 7)

    def scatter_all(half):
        for p in range(NZ):
            wg_out[half, p] = grad_acc[p * PART:(p + 1) * PART, :].astype(BF16)
        for dz in zorder:
            scatter(half, dz).start()
        return grad_acc[pl.ds(pl.multiple_of(dom * PART, 8), PART), :]

    def spread_all(half, own):
        for dz in reversed(zorder):
            scatter(half, dz).wait_recv()
            own = own + wg_in[half, dz].astype(F32)
        wg_all[half, dom] = own.astype(BF16)
        for dz in zorder:
            spread(half, dz, dom).start()

    forward(0)
    forward(1)
    relay(0)
    gradient(0)
    first = scatter_all(0)
    relay(1)
    gradient(1)
    second = scatter_all(1)
    spread_all(0, first)
    spread_all(1, second)

    def drain(step, carry):
        pair_copy(step).wait_send()
        return carry

    lax.fori_loop(0, 16, drain, 0)
    for step in range(16):
        if step % 4 < 3:
            x_copy(step, 1).wait_send()
        if step < 12:
            y_copy(step, 1).wait_send()
    for slot in range(3):
        turn_copy(0, slot, 1).wait_send()
        turn_copy(1, slot, 1).wait_send()
    for half in range(2):
        for d in range(1, 4):
            for line in range(5):
                over_x(half, me, line, d).wait_send()
                over_y(half, me, line, d).wait_send()
        for slot in range(16):
            to_core(half, me, slot).wait_send()
        for dz in range(1, NZ):
            scatter(half, dz).wait_send()
            spread(half, dz, dom).wait_send()
    for half in range(2):
        for dz in range(1, NZ):
            spread(half, dz, (dom + NZ - dz) % NZ).wait_recv()


def finish(act_in, wg_in, act_ref, grad_ref):
    act_ref[...] = act_in[...]
    for half in range(2):
        for p in range(NZ):
            grad_ref[p * PART:(p + 1) * PART, half * BLK:(half + 1) * BLK] = wg_in[half, p].astype(F32)


def body(
    features, proj_weight, source_block, slot_count, block_pattern, node_type, type_gain, cotangent
):
    vmem = pl.BlockSpec(memory_space=pltpu.VMEM)
    activations, parts = pl.pallas_call(
        kernel,
        out_shape=(
            jax.ShapeDtypeStruct((BLK, HID), BF16),
            jax.ShapeDtypeStruct((2, NZ, PART, BLK), BF16),
        ),
        in_specs=[pl.BlockSpec(memory_space=pl.ANY)] * 8,
        out_specs=(vmem, vmem),
        scratch_shapes=[
            pltpu.VMEM((PB * BLK, BLK), BF16),
            pltpu.VMEM((REL, BLK, HID), BF16),
            pltpu.SMEM((REL, SLOTS, PB), jnp.int32),
            pltpu.SMEM((REL, PB), jnp.int32),
            pltpu.VMEM((PB, REL, SLOTS, 8, BLK), jnp.int32),
            pltpu.VMEM((1, BLK), jnp.int32),
            pltpu.VMEM((NTYPES, HID), F32),
            pltpu.VMEM((BLK, HID), BF16),
            pltpu.SemaphoreType.DMA((8,)),
            pltpu.VMEM((PB, BLK, BLK), BF16),
            pltpu.VMEM((PB, BLK, BLK), BF16),
            pltpu.VMEM((HID, REL * BLK), BF16),
            pltpu.VMEM((PB, REL * BLK, BLK), BF16),
            pltpu.VMEM((16, HID, BLK), F32),
            pltpu.VMEM((3, BLK, BLK), F32),
            pltpu.VMEM((16, HID, BLK), BF16),
            pltpu.VMEM((16, HID, BLK), BF16),
            pltpu.VMEM((16, BLK, BLK), BF16),
            pltpu.VMEM((16, BLK, BLK), BF16),
            pltpu.VMEM((16, BLK, BLK), BF16),
            pltpu.VMEM((16, BLK, BLK), BF16),
            pltpu.VMEM((2, 3, BLK, BLK), BF16),
            pltpu.VMEM((2, 3, BLK, BLK), BF16),
            pltpu.VMEM((2, PB, BLK, BLK), BF16),
            pltpu.VMEM((REL * BLK, BLK), F32),
            pltpu.VMEM((2, NZ, PART, BLK), BF16),
            pltpu.VMEM((2, NZ, PART, BLK), BF16),
            pltpu.SemaphoreType.DMA((16,)),
            pltpu.SemaphoreType.DMA((16,)),
            pltpu.SemaphoreType.DMA((16,)),
            pltpu.SemaphoreType.DMA((16,)),
            pltpu.SemaphoreType.DMA((16,)),
            pltpu.SemaphoreType.DMA((16,)),
            pltpu.SemaphoreType.DMA((2, 3)),
            pltpu.SemaphoreType.DMA((2, 3)),
            pltpu.SemaphoreType.DMA((2, 5, 4)),
            pltpu.SemaphoreType.DMA((2, 5, 4)),
            pltpu.SemaphoreType.DMA((2, 5, 4)),
            pltpu.SemaphoreType.DMA((2, 5, 4)),
            pltpu.SemaphoreType.DMA((2, 16)),
            pltpu.SemaphoreType.DMA((2, 16)),
            pltpu.SemaphoreType.DMA((2, NZ)),
            pltpu.SemaphoreType.DMA((2, NZ)),
            pltpu.SemaphoreType.DMA((2, NZ)),
            pltpu.SemaphoreType.DMA((2, NZ)),
        ],
        compiler_params=pltpu.CompilerParams(
            collective_id=0, has_side_effects=True, vmem_limit_bytes=60 * 1024 * 1024
        ),
        name="graph_conv",
    )(
        features,
        proj_weight,
        jnp.transpose(source_block, (1, 2, 0)),
        jnp.transpose(slot_count, (1, 0)),
        block_pattern,
        node_type.reshape(1, BLK),
        type_gain,
        cotangent,
    )
    activations, grad = pl.pallas_call(
        finish,
        out_shape=(
            jax.ShapeDtypeStruct((BLK, HID), BF16),
            jax.ShapeDtypeStruct((REL * BLK, HID), F32),
        ),
        in_specs=[vmem, vmem],
        out_specs=(vmem, vmem),
        name="finish",
    )(activations, parts)
    return activations, grad.reshape(REL, BLK, HID)


def solution(mesh):
    placed = (
        P("dom", "feat"),
        P(None, "feat", None),
        P("dom", None, None),
        P("dom", None),
        P("dom", None, None, None, None),
        P(("dom", "feat")),
        P(),
        P(("dom", "feat"), None),
    )
    return jax.shard_map(
        body,
        mesh=mesh,
        in_specs=placed,
        out_specs=(P(("dom", "feat"), None), P(None, "feat", None)),
        check_vma=False,
    )
```

time: 70.7 us -> 61.3 us (0.87)
  the two profiles are of different devices: /device:TPU:8 before, /device:TPU:1 now
where the time goes in v2:
time: 61.3 us; the launch traced here: 61.2 us
  Pallas kernels  60.5 us (99%)
  between operations  0.64 us (1%)
    pallas_call x1, Pallas kernels, body(): pl.pallas_call(kernel, out_shape=(jax.ShapeDtypeStruct((BLK, HID), BF16),...  58.8 us
    pallas_call x1, Pallas kernels, body(): pl.pallas_call(finish, out_shape=(jax.ShapeDtypeStruct((BLK, HID), BF16),...  1.74 us

profile of v2, /device:TPU:1, one launch (start us, length us, event | category | flops | bytes accessed | tf_op | source)
XLA Modules:
  0.0 61.2 jit_solution(4799126564463018088)
XLA Ops:
  0.6 58.8 %graph_conv.1 = (bf16[128,256]{1,0:T(8,128)(2,1)}, bf16[2,8,48,128]{3,2,1,0:T(8,128)(2,1)}) custom-call(bf16[4096,128]{1,0:T(8,128)(2,1)} %feat_hbm.1, bf16[3,128,256]{2,1,0:T(8,128)(2,1)} %weight_hbm.1, s32[3,4,32]{2,1,0:T(4,128)} %bitcast.4, s32[3,32]{1,0:T(4,128)} %bitcast.5, s32[32,3,4,8,128]{4,3,2,1,0:T(8,128)} %pattern_hbm.1, s32[1,128]{1,0:T(1,128)} %bitcast.6, ...), custom_call_target="tpu_custom_call" | custom-call | tf_op jit(solution)/shard_map/graph_conv/pallas_call | solution.py:483
  59.4 1.7 %finish.1 = (bf16[128,256]{1,0:T(8,128)(2,1)}, f32[384,256]{1,0:T(8,128)}) custom-call(bf16[128,256]{1,0:T(8,128)(2,1)} %get-tuple-element.6.act_in, bf16[2,8,48,128]{3,2,1,0:T(8,128)(2,1)} %get-tuple-element.7.wg_in), custom_call_target="tpu_custom_call" | custom-call | tf_op jit(solution)/shard_map/finish/pallas_call | solution.py:552

commit v3 on v2

--- a/solution.py
+++ b/solution.py
@@ -92,10 +92,16 @@
     def device_at(dy, dx):
         return (((y + dy) % 4) * 4 + (x + dx) % 4) * 2 + core
 
+    def piece_of(ref, n):
+        return ref.at[pl.ds(n * 1024, 1024)]
+
     loads = [
         pltpu.make_async_copy(src, dst, load_sem.at[n])
         for n, (src, dst) in enumerate((
-            (feat_hbm, feat_ref),
+            (piece_of(feat_hbm, 0), piece_of(feat_ref, 0)),
+            (piece_of(feat_hbm, 1), piece_of(feat_ref, 1)),
+            (piece_of(feat_hbm, 2), piece_of(feat_ref, 2)),
+            (piece_of(feat_hbm, 3), piece_of(feat_ref, 3)),
             (weight_hbm, weight_ref),
             (source_hbm, source_ref),
             (count_hbm, count_ref),
@@ -114,8 +120,9 @@
         pl.semaphore_signal(barrier, inc=1, device_id=dest, device_id_type=MESH)
 
     greet(at_feat(partner))
-    for off in range(1, 16):
-        greet(at_feat(device_at(off // 4, off % 4)))
+    for d in range(1, 4):
+        greet(at_feat(device_at(0, d)))
+        greet(at_feat(device_at(d, 0)))
     for dz in range(1, NZ):
         greet(((dom + dz) % NZ, me))
 
@@ -125,28 +132,27 @@
     perm = jnp.where(row == (col % 8) * 16 + col // 8, scale, 0.0).astype(BF16)
     eye = jnp.where(row == col, 1.0, 0.0).astype(BF16)
 
-    loads[0].wait()
-    loads[1].wait()
+    for n in range(4):
+        loads[n].wait()
+        flipped = lax.dot_general(
+            eye,
+            feat_ref[n * 1024:(n + 1) * 1024],
+            (((1,), (1,)), ((), ())),
+            preferred_element_type=F32,
+        ).astype(BF16)
+        blocks = [flipped[:, k * BLK:(k + 1) * BLK] for k in range(8)]
+        for k in range(8):
+            self_t[n * 8 + k] = blocks[k]
+        moved = jnp.dot(jnp.concatenate(blocks, axis=0), perm, preferred_element_type=F32)
+        perm_t[n * 8:(n + 1) * 8] = moved.astype(BF16).reshape(8, BLK, BLK)
+    loads[4].wait()
     for r in range(REL):
         for half in range(2):
             piece = weight_ref[r, :, half * BLK:(half + 1) * BLK]
             weight_t[half * BLK:(half + 1) * BLK, r * BLK:(r + 1) * BLK] = (
                 piece.astype(F32).T.astype(BF16)
             )
-
-    def prepare(i, carry):
-        for k in range(4):
-            b = i * 4 + k
-            rows = feat_ref[pl.ds(pl.multiple_of(b * BLK, BLK), BLK), :]
-            flipped = lax.dot_general(
-                eye, rows, (((1,), (1,)), ((), ())), preferred_element_type=F32
-            ).astype(BF16)
-            self_t[b] = flipped
-            perm_t[b] = jnp.dot(flipped, perm, preferred_element_type=F32).astype(BF16)
-        return carry
-
-    lax.fori_loop(0, PB // 4, prepare, 0)
-    for load in loads[2:]:
+    for load in loads[5:]:
         load.wait()
 
     def mix(b):
@@ -263,7 +269,7 @@
             mine = mine + y_in[4 * group + k].astype(F32)
         return mine
 
-    pl.semaphore_wait(barrier, 1 + 15 + NZ - 1)
+    pl.semaphore_wait(barrier, 1 + 6 + NZ - 1)
     project(0)
     project(1)
 
@@ -373,13 +379,6 @@
             over_y(half, block, 1 + dx, dy).wait_recv()
         return block
 
-    def add_grad(half, block, slot):
-        twin = block + 1 - 2 * core
-        to_core(half, twin, slot).wait_recv()
-        lhs = jnp.concatenate([mixed_t[block], mixed_t[twin]], axis=1)
-        rhs = jnp.concatenate([slope_all[half, block], slope_all[half, twin]], axis=0)
-        return jnp.dot(lhs, rhs, preferred_element_type=F32)
-
     order = [(0, 1), (0, 3), (1, 0), (3, 0), (0, 2), (2, 0), (1, 1), (1, 3), (3, 1), (3, 3),
              (1, 2), (2, 1), (3, 2), (2, 3), (2, 2)]
 
@@ -389,9 +388,24 @@
             to_core(half, block, dy * 4 + dx).start()
 
     def gradient(half):
-        grad_acc[...] = add_grad(half, me, 0)
-        for dy, dx in order:
-            grad_acc[...] += add_grad(half, device_at(4 - dy, 4 - dx), dy * 4 + dx)
+        places = [(0, 0)] + order
+        for chunk in range(4):
+            lhs, rhs = [], []
+            for dy, dx in places[4 * chunk:4 * chunk + 4]:
+                block = device_at((4 - dy) % 4, (4 - dx) % 4)
+                twin = block + 1 - 2 * core
+                to_core(half, twin, dy * 4 + dx).wait_recv()
+                lhs += [mixed_t[block], mixed_t[twin]]
+                rhs += [slope_all[half, block], slope_all[half, twin]]
+            product = jnp.dot(
+                jnp.concatenate(lhs, axis=1),
+                jnp.concatenate(rhs, axis=0),
+                preferred_element_type=F32,
+            )
+            if chunk == 0:
+                grad_acc[...] = product
+            else:
+                grad_acc[...] += product
 
     def scatter(half, dz):
         return pltpu.make_async_remote_copy(
@@ -497,7 +511,7 @@
             pltpu.VMEM((1, BLK), jnp.int32),
             pltpu.VMEM((NTYPES, HID), F32),
             pltpu.VMEM((BLK, HID), BF16),
-            pltpu.SemaphoreType.DMA((8,)),
+            pltpu.SemaphoreType.DMA((11,)),
             pltpu.VMEM((PB, BLK, BLK), BF16),
             pltpu.VMEM((PB, BLK, BLK), BF16),
             pltpu.VMEM((HID, REL * BLK), BF16),

time: 61.3 us -> 56.9 us (0.928)
  Pallas kernels: 60.5 us -> 56.1 us
    pallas_call x1, Pallas kernels: 58.8 us -> 54.4 us  [body(): pl.pallas_call(kernel, out_shape=(jax.ShapeDtypeStruct((BLK, HID), BF16),...]
where the time goes in v3:
time: 56.9 us; the launch traced here: 56.8 us
  Pallas kernels  56.1 us (99%)
  between operations  0.64 us (1%)
    pallas_call x1, Pallas kernels, body(): pl.pallas_call(kernel, out_shape=(jax.ShapeDtypeStruct((BLK, HID), BF16),...  54.4 us
    pallas_call x1, Pallas kernels, body(): pl.pallas_call(finish, out_shape=(jax.ShapeDtypeStruct((BLK, HID), BF16),...  1.74 us

profile of v3, /device:TPU:1, one launch (start us, length us, event | category | flops | bytes accessed | tf_op | source)
XLA Modules:
  0.0 56.8 jit_solution(13382652017140853729)
XLA Ops:
  0.6 54.4 %graph_conv.1 = (bf16[128,256]{1,0:T(8,128)(2,1)}, bf16[2,8,48,128]{3,2,1,0:T(8,128)(2,1)}) custom-call(bf16[4096,128]{1,0:T(8,128)(2,1)} %feat_hbm.1, bf16[3,128,256]{2,1,0:T(8,128)(2,1)} %weight_hbm.1, s32[3,4,32]{2,1,0:T(4,128)} %bitcast.4, s32[3,32]{1,0:T(4,128)} %bitcast.5, s32[32,3,4,8,128]{4,3,2,1,0:T(8,128)} %pattern_hbm.1, s32[1,128]{1,0:T(1,128)} %bitcast.6, ...), custom_call_target="tpu_custom_call" | custom-call | tf_op jit(solution)/shard_map/graph_conv/pallas_call | solution.py:497
  55.0 1.7 %finish.1 = (bf16[128,256]{1,0:T(8,128)(2,1)}, f32[384,256]{1,0:T(8,128)}) custom-call(bf16[128,256]{1,0:T(8,128)(2,1)} %get-tuple-element.6.act_in, bf16[2,8,48,128]{3,2,1,0:T(8,128)(2,1)} %get-tuple-element.7.wg_in), custom_call_target="tpu_custom_call" | custom-call | tf_op jit(solution)/shard_map/finish/pallas_call | solution.py:566

commit v4 on v3

--- a/solution.py
+++ b/solution.py
@@ -228,16 +228,18 @@
             device_id_type=MESH,
         )
 
+    def mix_both(step):
+        mine = target(step)
+        mix(mine)
+        mix(mine + 1 - 2 * core)
+
     def project(step):
         mine = target(step)
         other = mine + 1 - 2 * core
-        mix(mine)
-        mix(other)
         both = jnp.concatenate([mixed_t[mine], mixed_t[other]], axis=1)
         part = jnp.dot(weight_t[...], both, preferred_element_type=F32)
         own_part[step] = part[:, :BLK]
         pair_out[step] = part[:, BLK:].astype(BF16)
-        pair_copy(step).start()
 
     def top_sum(step):
         return own_part[step, :BLK] + pair_in[step, :BLK].astype(F32)
@@ -270,14 +272,21 @@
         return mine
 
     pl.semaphore_wait(barrier, 1 + 6 + NZ - 1)
+    mix_both(0)
     project(0)
+    mix_both(1)
+    pair_copy(0).start()
     project(1)
+    mix_both(2)
+    pair_copy(1).start()
 
     def four(group, carry):
         dy = shift(group)
         for k in range(4):
             step = 4 * group + k
             project(step + 2)
+            mix_both(step + 3)
+            pair_copy(step + 2).start()
             pair_copy(step).wait_recv()
             if k < 3:
                 send_top(step, k)
@@ -295,6 +304,9 @@
         step = 12 + k
         if k < 2:
             project(step + 2)
+            if k < 1:
+                mix_both(step + 3)
+            pair_copy(step + 2).start()
         pair_copy(step).wait_recv()
         if k < 3:
             send_top(step, k)
@@ -302,25 +314,6 @@
             turn_copy(1, k, DXS[k]).start()
         if k == 2:
             send_row(2, 1)
-    top = row_sum(3, top_sum(15))
-    low = column_sum(3, low_sum(15))
-    for slot in range(3):
-        turn_copy(0, slot, 1).wait_recv()
-        top = top + turn_in[0, slot].astype(F32)
-        turn_copy(1, slot, 1).wait_recv()
-        low = low + turn_in[1, slot].astype(F32)
-
-    types = jnp.broadcast_to(type_ref[...].astype(F32), (BLK, BLK)).T
-    for half in range(2):
-        cols = slice(half * BLK, (half + 1) * BLK)
-        pre = (top, low)[half].T
-        gains = gain_ref[:, cols]
-        gain = jnp.where(types == 0.0, gains[0:1], jnp.where(types == 1.0, gains[1:2], gains[2:3]))
-        sig = jax.nn.sigmoid(pre)
-        act_ref[:, cols] = (pre * sig * gain).astype(BF16)
-        slope = cot_ref[:, cols].astype(F32) * gain * (sig * (1.0 + pre * (1.0 - sig)))
-        slope_all[half, me] = slope.astype(BF16)
-
     def to_core(half, block, slot):
         return pltpu.make_async_remote_copy(
             src_ref=slope_all.at[half, block],
@@ -353,7 +346,20 @@
             device_id_type=MESH,
         )
 
+    types = jnp.broadcast_to(type_ref[...].astype(F32), (BLK, BLK)).T
     for half in range(2):
+        total = row_sum(3, top_sum(15)) if half == 0 else column_sum(3, low_sum(15))
+        for slot in range(3):
+            turn_copy(half, slot, 1).wait_recv()
+            total = total + turn_in[half, slot].astype(F32)
+        cols = slice(half * BLK, (half + 1) * BLK)
+        pre = total.T
+        gains = gain_ref[:, cols]
+        gain = jnp.where(types == 0.0, gains[0:1], jnp.where(types == 1.0, gains[1:2], gains[2:3]))
+        sig = jax.nn.sigmoid(pre)
+        slope = cot_ref[:, cols].astype(F32) * gain * (sig * (1.0 + pre * (1.0 - sig)))
+        slope_all[half, me] = slope.astype(BF16)
+        act_ref[:, cols] = (pre * sig * gain).astype(BF16)
         for line in range(2):
             for d in DXS[:3]:
                 over_x(half, me, line, d).start()

time: 56.9 us -> 55.5 us (0.975)
  Pallas kernels: 56.1 us -> 54.7 us
    pallas_call x1, Pallas kernels: 54.4 us -> 53 us  [body(): pl.pallas_call(kernel, out_shape=(jax.ShapeDtypeStruct((BLK, HID), BF16),...]
where the time goes in v4:
time: 55.5 us; the launch traced here: 55.4 us
  Pallas kernels  54.7 us (99%)
  between operations  0.64 us (1%)
    pallas_call x1, Pallas kernels, body(): pl.pallas_call(kernel, out_shape=(jax.ShapeDtypeStruct((BLK, HID), BF16),...  53 us
    pallas_call x1, Pallas kernels, body(): pl.pallas_call(finish, out_shape=(jax.ShapeDtypeStruct((BLK, HID), BF16),...  1.74 us

profile of v4, /device:TPU:1, one launch (start us, length us, event | category | flops | bytes accessed | tf_op | source)
XLA Modules:
  0.0 55.4 jit_solution(1832123654710317312)
XLA Ops:
  0.6 53.0 %graph_conv.1 = (bf16[128,256]{1,0:T(8,128)(2,1)}, bf16[2,8,48,128]{3,2,1,0:T(8,128)(2,1)}) custom-call(bf16[4096,128]{1,0:T(8,128)(2,1)} %feat_hbm.1, bf16[3,128,256]{2,1,0:T(8,128)(2,1)} %weight_hbm.1, s32[3,4,32]{2,1,0:T(4,128)} %bitcast.4, s32[3,32]{1,0:T(4,128)} %bitcast.5, s32[32,3,4,8,128]{4,3,2,1,0:T(8,128)} %pattern_hbm.1, s32[1,128]{1,0:T(1,128)} %bitcast.6, ...), custom_call_target="tpu_custom_call" | custom-call | tf_op jit(solution)/shard_map/graph_conv/pallas_call | solution.py:503
  53.6 1.7 %finish.1 = (bf16[128,256]{1,0:T(8,128)(2,1)}, f32[384,256]{1,0:T(8,128)}) custom-call(bf16[128,256]{1,0:T(8,128)(2,1)} %get-tuple-element.6.act_in, bf16[2,8,48,128]{3,2,1,0:T(8,128)(2,1)} %get-tuple-element.7.wg_in), custom_call_target="tpu_custom_call" | custom-call | tf_op jit(solution)/shard_map/finish/pallas_call | solution.py:572

commit v5 on v4

--- a/solution.py
+++ b/solution.py
@@ -506,7 +506,7 @@
             jax.ShapeDtypeStruct((BLK, HID), BF16),
             jax.ShapeDtypeStruct((2, NZ, PART, BLK), BF16),
         ),
-        in_specs=[pl.BlockSpec(memory_space=pl.ANY)] * 8,
+        in_specs=[pl.BlockSpec(memory_space=pltpu.HBM)] * 8,
         out_specs=(vmem, vmem),
         scratch_shapes=[
             pltpu.VMEM((PB * BLK, BLK), BF16),
@@ -556,10 +556,10 @@
             pltpu.SemaphoreType.DMA((2, NZ)),
         ],
         compiler_params=pltpu.CompilerParams(
-            collective_id=0, has_side_effects=True, vmem_limit_bytes=60 * 1024 * 1024
+            collective_id=0, has_side_effects=True, vmem_limit_bytes=40 * 1024 * 1024
         ),
         name="graph_conv",
-    )(
+    )(*(pltpu.with_memory_space_constraint(v, pltpu.HBM) for v in (
         features,
         proj_weight,
         jnp.transpose(source_block, (1, 2, 0)),
@@ -568,7 +568,7 @@
         node_type.reshape(1, BLK),
         type_gain,
         cotangent,
-    )
+    )))
     activations, grad = pl.pallas_call(
         finish,
         out_shape=(
@@ -577,6 +577,7 @@
         ),
         in_specs=[vmem, vmem],
         out_specs=(vmem, vmem),
+        compiler_params=pltpu.CompilerParams(vmem_limit_bytes=4 * 1024 * 1024),
         name="finish",
     )(activations, parts)
     return activations, grad.reshape(REL, BLK, HID)

time: 55.5 us -> 53.8 us (0.969)
  Pallas kernels: 54.7 us -> 53.1 us
    pallas_call x1, Pallas kernels: 1.74 us -> 0.79 us  [body(): pl.pallas_call(finish, out_shape=(jax.ShapeDtypeStruct((BLK, HID), BF16),...]
    pallas_call x1, Pallas kernels: 53 us -> 52.3 us  [body(): pl.pallas_call(kernel, out_shape=(jax.ShapeDtypeStruct((BLK, HID), BF16),...]
where the time goes in v5:
time: 53.8 us; the launch traced here: 53.7 us
  Pallas kernels  53.1 us (99%)
  between operations  0.64 us (1%)
    pallas_call x1, Pallas kernels, body(): pl.pallas_call(kernel, out_shape=(jax.ShapeDtypeStruct((BLK, HID), BF16),...  52.3 us

profile of v5, /device:TPU:1, one launch (start us, length us, event | category | flops | bytes accessed | tf_op | source)
XLA Modules:
  0.0 53.7 jit_solution(18003723702899983139)
XLA Ops:
  0.6 52.3 %graph_conv.1 = (bf16[128,256]{1,0:T(8,128)(2,1)S(1)}, bf16[2,8,48,128]{3,2,1,0:T(8,128)(2,1)S(1)}) custom-call(bf16[4096,128]{1,0:T(8,128)(2,1)} %feat_hbm.1, bf16[3,128,256]{2,1,0:T(8,128)(2,1)} %weight_hbm.1, s32[3,4,32]{2,1,0:T(4,128)} %bitcast.4, s32[3,32]{1,0:T(4,128)} %bitcast.5, s32[32,3,4,8,128]{4,3,2,1,0:T(8,128)} %pattern_hbm.1, ...), custom_call_target="tpu_custom_call" | custom-call | tf_op jit(solution)/shard_map/graph_conv/pallas_call | solution.py:503
  52.9 0.8 %finish.1 = (bf16[128,256]{1,0:T(8,128)(2,1)}, f32[384,256]{1,0:T(8,128)}) custom-call(bf16[128,256]{1,0:T(8,128)(2,1)S(1)} %get-tuple-element.6.act_in, bf16[2,8,48,128]{3,2,1,0:T(8,128)(2,1)S(1)} %get-tuple-element.7.wg_in), custom_call_target="tpu_custom_call" | custom-call | tf_op jit(solution)/shard_map/finish/pallas_call | solution.py:572

commit v6 on v5

--- a/solution.py
+++ b/solution.py
@@ -388,30 +388,37 @@
     order = [(0, 1), (0, 3), (1, 0), (3, 0), (0, 2), (2, 0), (1, 1), (1, 3), (3, 1), (3, 3),
              (1, 2), (2, 1), (3, 2), (2, 3), (2, 2)]
 
-    def relay(half):
-        for dy, dx in order:
-            block = arrived(half, dy, dx)
-            to_core(half, block, dy * 4 + dx).start()
+    places = [(0, 0)] + order
+
+    def relay(half, chunk):
+        for dy, dx in places[4 * chunk:4 * chunk + 4]:
+            if (dy, dx) != (0, 0):
+                to_core(half, arrived(half, dy, dx), dy * 4 + dx).start()
+
+    def multiply(half, chunk):
+        lhs, rhs = [], []
+        for dy, dx in places[4 * chunk:4 * chunk + 4]:
+            block = device_at((4 - dy) % 4, (4 - dx) % 4)
+            twin = block + 1 - 2 * core
+            to_core(half, twin, dy * 4 + dx).wait_recv()
+            lhs += [mixed_t[block], mixed_t[twin]]
+            rhs += [slope_all[half, block], slope_all[half, twin]]
+        product = jnp.dot(
+            jnp.concatenate(lhs, axis=1),
+            jnp.concatenate(rhs, axis=0),
+            preferred_element_type=F32,
+        )
+        if chunk == 0:
+            grad_acc[...] = product
+        else:
+            grad_acc[...] += product
 
     def gradient(half):
-        places = [(0, 0)] + order
+        relay(half, 0)
         for chunk in range(4):
-            lhs, rhs = [], []
-            for dy, dx in places[4 * chunk:4 * chunk + 4]:
-                block = device_at((4 - dy) % 4, (4 - dx) % 4)
-                twin = block + 1 - 2 * core
-                to_core(half, twin, dy * 4 + dx).wait_recv()
-                lhs += [mixed_t[block], mixed_t[twin]]
-                rhs += [slope_all[half, block], slope_all[half, twin]]
-            product = jnp.dot(
-                jnp.concatenate(lhs, axis=1),
-                jnp.concatenate(rhs, axis=0),
-                preferred_element_type=F32,
-            )
-            if chunk == 0:
-                grad_acc[...] = product
-            else:
-                grad_acc[...] += product
+            if chunk < 3:
+                relay(half, chunk + 1)
+            multiply(half, chunk)
 
     def scatter(half, dz):
         return pltpu.make_async_remote_copy(
@@ -452,10 +459,8 @@
 
     forward(0)
     forward(1)
-    relay(0)
     gradient(0)
     first = scatter_all(0)
-    relay(1)
     gradient(1)
     second = scatter_all(1)
     spread_all(0, first)

time: 53.8 us -> 53.5 us (level)
  the two profiles are of different devices: /device:TPU:1 before, /device:TPU:8 now
where the time goes in v6:
time: 53.5 us; the launch traced here: 53.4 us
  Pallas kernels  52.7 us (99%)
  between operations  0.64 us (1%)
    pallas_call x1, Pallas kernels, body(): pl.pallas_call(kernel, out_shape=(jax.ShapeDtypeStruct((BLK, HID), BF16),...  51.9 us

profile of v6, /device:TPU:8, one launch (start us, length us, event | category | flops | bytes accessed | tf_op | source)
XLA Modules:
  0.0 53.4 jit_solution(11845917111148511714)
XLA Ops:
  0.6 51.9 %graph_conv.1 = (bf16[128,256]{1,0:T(8,128)(2,1)S(1)}, bf16[2,8,48,128]{3,2,1,0:T(8,128)(2,1)S(1)}) custom-call(bf16[4096,128]{1,0:T(8,128)(2,1)} %feat_hbm.1, bf16[3,128,256]{2,1,0:T(8,128)(2,1)} %weight_hbm.1, s32[3,4,32]{2,1,0:T(4,128)} %bitcast.4, s32[3,32]{1,0:T(4,128)} %bitcast.5, s32[32,3,4,8,128]{4,3,2,1,0:T(8,128)} %pattern_hbm.1, ...), custom_call_target="tpu_custom_call" | custom-call | tf_op jit(solution)/shard_map/graph_conv/pallas_call | solution.py:508
  52.6 0.8 %finish.1 = (bf16[128,256]{1,0:T(8,128)(2,1)}, f32[384,256]{1,0:T(8,128)}) custom-call(bf16[128,256]{1,0:T(8,128)(2,1)S(1)} %get-tuple-element.6.act_in, bf16[2,8,48,128]{3,2,1,0:T(8,128)(2,1)S(1)} %get-tuple-element.7.wg_in), custom_call_target="tpu_custom_call" | custom-call | tf_op jit(solution)/shard_map/finish/pallas_call | solution.py:577
